TPU v7x, 256 devices: a whole 4x4x8 slice. The times are simulated.
256 devices in a mesh: row: 32 (over y, x, core), col: 8 (over z).
Axes of the slice: x: 4, y: 4, z: 8, core: 2. Of those that a mesh axis runs over, the one named last changes fastest.
Arguments:
- diag: float32 [4, 1024, 1024], P(None, 'row'), as said below
- panel_rows: float32 [64, 8, 64, 1024], P('row', None, None, 'col')
- panel_cols: float32 [8, 8, 64, 1024], P('col', None, 'row')
- trailing: float32 [64, 8, 8, 64, 1024], P('row', 'col')
- sketch: float32 [64, 1024], replicated, may hold values from -6 to 6
- panel_rank: int32 [64], P('row'), may hold values from 16 to 64
- col_rank: int32 [8], P('col'), may hold values from 16 to 64
- tile_rank: int32 [64, 8], P('row', 'col'), may hold values from 32 to 64
- keep_rank: int32 [64, 8], P('row', 'col'), may hold values from 8 to 32
Outputs:
- new_tiles: float32 [64, 8, 8, 64, 1024], P('row', 'col')
Inputs may be any that keep to these rules, and one draw needn't show every extreme that they name: `keep_rank`: recompression ranks, never above the tile's rank. diag[0] is symmetric positive definite with smallest eigenvalue 0.5 or more; the tangents are symmetric.
All inputs are finite; a program needn't handle non-finite values.
Results may differ from a plain program's by a relative error of at most 0.0003.
Values sent between devices are 32-bit elements; how exact they have to be, the bound alone decides.
A program may use at most 192 MiB of HBM per device.

v0:
```python
import math
import jax
import jax.numpy as jnp
from jax import lax
from jax.sharding import PartitionSpec as P

HIGHEST_PRECISION = lax.Precision.HIGHEST


def highest_accuracy(left, right):
    return jnp.dot(left, right, precision=HIGHEST_PRECISION, preferred_element_type=jnp.float32)


def rank_mask(rank_values, rank_count):
    return (jnp.arange(rank_count, dtype=jnp.int32) < rank_values[..., None]).astype(jnp.float32)


def inverse_apply(lower_factor, rank_rows):
    half_solved = jax.scipy.linalg.solve_triangular(lower_factor, rank_rows.T, lower=True)
    full_solved = jax.scipy.linalg.solve_triangular(lower_factor, half_solved, lower=True, trans=1)
    return full_solved.T


def sketch_apply(active_sketch, previous_left_factor, previous_right_factor, u_row, mix_in, u_col):
    return highest_accuracy(
        highest_accuracy(active_sketch, previous_right_factor.T), previous_left_factor
    ) - highest_accuracy(
        highest_accuracy(highest_accuracy(active_sketch, u_col.T), mix_in.T), u_row
    )


def basis_apply(
    row_basis_matrix, previous_left_factor, previous_right_factor, u_row, mix_in, u_col
):
    return highest_accuracy(
        highest_accuracy(row_basis_matrix, previous_left_factor.T), previous_right_factor
    ) - highest_accuracy(
        highest_accuracy(highest_accuracy(row_basis_matrix, u_row.T), mix_in), u_col
    )


def compress_all(
    previous_left_factor,
    previous_right_factor,
    u_row,
    mix_in,
    u_col,
    du_old,
    dv_old,
    du_row,
    dmix_in,
    du_col,
    active_sketch,
    live_mask,
):
    sketched = sketch_apply(
        active_sketch, previous_left_factor, previous_right_factor, u_row, mix_in, u_col
    )
    gram_matrix = highest_accuracy(sketched, sketched.T) + jnp.diag(1.0 - live_mask)
    factor = jnp.linalg.cholesky(gram_matrix)
    row_basis_matrix = jax.scipy.linalg.solve_triangular(factor, sketched, lower=True)
    coefficients = basis_apply(
        row_basis_matrix, previous_left_factor, previous_right_factor, u_row, mix_in, u_col
    )
    up_scale = math.sqrt(previous_left_factor.shape[1])
    down_scale = math.sqrt(previous_left_factor.shape[0])

    def tangent_direction(
        previous_left_derivative,
        previous_right_derivative,
        row_left_derivative,
        mixing_derivative,
        column_left_derivative,
    ):
        sketch_derivative = highest_accuracy(
            highest_accuracy(active_sketch, previous_right_derivative.T), previous_left_factor
        ) + highest_accuracy(
            highest_accuracy(active_sketch, previous_right_factor.T), previous_left_derivative
        )
        sketch_derivative = sketch_derivative - highest_accuracy(
            highest_accuracy(highest_accuracy(active_sketch, column_left_derivative.T), mix_in.T),
            u_row,
        )
        sketch_derivative = sketch_derivative - highest_accuracy(
            highest_accuracy(highest_accuracy(active_sketch, u_col.T), mixing_derivative.T), u_row
        )
        sketch_derivative = sketch_derivative - highest_accuracy(
            highest_accuracy(highest_accuracy(active_sketch, u_col.T), mix_in.T),
            row_left_derivative,
        )
        d_gram = highest_accuracy(sketch_derivative, sketched.T) + highest_accuracy(
            sketched, sketch_derivative.T
        )
        inner = jax.scipy.linalg.solve_triangular(factor, d_gram, lower=True)
        middle = jax.scipy.linalg.solve_triangular(factor, inner.T, lower=True)
        lower_part = jnp.tril(middle) - 0.5 * jnp.diag(jnp.diagonal(middle))
        d_factor = highest_accuracy(factor, lower_part)
        d_basis = jax.scipy.linalg.solve_triangular(
            factor, sketch_derivative - highest_accuracy(d_factor, row_basis_matrix), lower=True
        )
        coefficient_derivative = basis_apply(
            d_basis, previous_left_factor, previous_right_factor, u_row, mix_in, u_col
        )
        coefficient_derivative = (
            coefficient_derivative
            + highest_accuracy(
                highest_accuracy(row_basis_matrix, previous_left_derivative.T),
                previous_right_factor,
            )
            + highest_accuracy(
                highest_accuracy(row_basis_matrix, previous_left_factor.T),
                previous_right_derivative,
            )
        )
        coefficient_derivative = coefficient_derivative - highest_accuracy(
            highest_accuracy(highest_accuracy(row_basis_matrix, row_left_derivative.T), mix_in),
            u_col,
        )
        coefficient_derivative = coefficient_derivative - highest_accuracy(
            highest_accuracy(highest_accuracy(row_basis_matrix, u_row.T), mixing_derivative), u_col
        )
        coefficient_derivative = coefficient_derivative - highest_accuracy(
            highest_accuracy(highest_accuracy(row_basis_matrix, u_row.T), mix_in),
            column_left_derivative,
        )
        return (d_basis * up_scale, coefficient_derivative / down_scale)

    tangent_basis, tangent_coeff = jax.vmap(tangent_direction)(
        du_old, dv_old, du_row, dmix_in, du_col
    )
    return (row_basis_matrix * up_scale, coefficients / down_scale, tangent_basis, tangent_coeff)


def update_tile(
    row_tile, row_solved, col_tile, col_solved, col_products, old_tile, tile_mask, keep_mask, sketch
):
    old_tile = old_tile * tile_mask[None, :, None]
    mixing = highest_accuracy(row_tile[4], col_solved.T)
    tangent_mix = jnp.stack(
        [
            highest_accuracy(row_tile[5 + direction], col_solved.T)
            + highest_accuracy(row_solved, col_tile[5 + direction].T)
            - highest_accuracy(row_solved, col_products[direction].T)
            for direction in range(3)
        ]
    )
    active_sketch = sketch * keep_mask[:, None]
    basis_out, coeff_out, tangent_basis, tangent_coeff = compress_all(
        old_tile[0],
        old_tile[4],
        row_tile[0],
        mixing,
        col_tile[0],
        old_tile[1:4],
        old_tile[5:8],
        row_tile[1:4],
        tangent_mix,
        col_tile[1:4],
        active_sketch,
        keep_mask,
    )
    return jnp.concatenate([basis_out[None], tangent_basis, coeff_out[None], tangent_coeff], axis=0)


def on_device(
    diag, panel_rows, panel_cols, trailing, sketch, panel_rank, col_rank, tile_rank, keep_rank
):
    rank_count = sketch.shape[0]
    tile_width = sketch.shape[1]
    gathered = lax.all_gather(diag, "row", axis=1, tiled=True)
    primal = gathered[0]
    lower_factor = jnp.linalg.cholesky(primal)
    rows_kept = (
        lax.all_gather(panel_rows, "col", axis=3, tiled=True)
        * rank_mask(panel_rank, rank_count)[:, None, :, None]
    )
    cols_kept = (
        lax.all_gather(panel_cols, "row", axis=2, tiled=True)
        * rank_mask(col_rank, rank_count)[:, None, :, None]
    )
    col_tile = cols_kept[0]
    col_solved = inverse_apply(lower_factor, col_tile[4])
    col_products = jnp.einsum("aj,tij->tai", col_solved, gathered[1:], precision=HIGHEST_PRECISION)
    local_rows = rows_kept.shape[0]
    row_solved = inverse_apply(lower_factor, rows_kept[:, 4].reshape(-1, tile_width)).reshape(
        local_rows, rank_count, tile_width
    )
    tile_live = rank_mask(tile_rank[:, 0], rank_count)
    keep_live = rank_mask(keep_rank[:, 0], rank_count)

    def one_tile(row_tile, row_z, old_tile, tile_mask, keep_mask):
        return update_tile(
            row_tile,
            row_z,
            col_tile,
            col_solved,
            col_products,
            old_tile,
            tile_mask,
            keep_mask,
            sketch,
        )

    updated = jax.vmap(one_tile)(rows_kept, row_solved, trailing[:, 0], tile_live, keep_live)
    return updated[:, None]


def solution(mesh):
    in_specs = (
        P(None, "row", None),
        P("row", None, None, "col"),
        P("col", None, "row", None),
        P("row", "col", None, None, None),
        P(),
        P("row"),
        P("col"),
        P("row", "col"),
        P("row", "col"),
    )
    out_specs = P("row", "col", None, None, None)
    return jax.shard_map(
        on_device, mesh=mesh, in_specs=in_specs, out_specs=out_specs, check_vma=False
    )
```

profile of v0, /device:TPU:1, one launch (start us, length us, event | category | flops | bytes accessed | tf_op | source)
XLA Modules:
  0.0 733.9 jit_solution(14539865115307290714)
XLA Ops:
  28.6 34.0 %all-gather.4.cloned.1.call-done = f32[1,8,64,1024]{3,1,0,2:T(8,128)} async-done(((f32[1,8,2,1024]{3,1,0,2:T(8,128)}), f32[1,8,64,1024]{3,1,0,2:T(8,128)}) %all-gather.4.cloned.1.call-update) | async-done | bytes 2097168 | tf_op jit(solution)/shard_map/all_gather | solution.py:178
  68.1 54.0 %all-gather.6.cloned.1.call-done = f32[2,8,64,1024]{3,2,0,1:T(8,128)} async-done(((f32[2,8,64,128]{3,2,0,1:T(8,128)}), f32[2,8,64,1024]{3,2,0,1:T(8,128)}) %all-gather.6.cloned.1.call-update) | async-done | bytes 4194320 | tf_op jit(solution)/shard_map/all_gather | solution.py:174
  130.6 74.5 %all-gather.8.cloned.1.call-done = f32[4,1024,1024]{2,0,1:T(4,128)} async-done(((f32[4,32,1024]{2,0,1:T(4,128)}), f32[4,1024,1024]{2,0,1:T(4,128)}) %all-gather.8.cloned.1.call-update) | async-done | bytes 16777232 | tf_op jit(solution)/shard_map/all_gather | solution.py:170
  213.8 11.4 %copy.214 = f32[1,1024,1024]{1,2,0:T(8,128)} copy(f32[1,1024,1024]{2,0,1:T(1,128)} %slice.584) | data formatting | bytes 8388608
  232.2 11.7 %cholesky.241 = f32[128,128]{1,0:T(8,128)S(1)} custom-call(f32[128,128]{1,0:T(8,128)S(1)} %cholesky.622), custom_call_target="Cholesky" | custom-call | tf_op jit(solution)/shard_map/jit(cholesky)/cholesky | solution.py:172
  243.9 9.8 %custom-call.86 = f32[1,128,128]{1,2,0:T(8,128)S(1)} custom-call(f32[1,128,128]{2,1,0:T(8,128)S(1)} %get-tuple-element.70), custom_call_target="InvertDiagBlocksLowerTriangular" | custom-call | tf_op jit(solution)/shard_map/jit(cholesky)/cholesky | solution.py:172
  260.2 11.8 %cholesky.264 = f32[128,128]{1,0:T(8,128)S(1)} custom-call(f32[128,128]{1,0:T(8,128)S(1)} %cholesky.626), custom_call_target="Cholesky" | custom-call | tf_op jit(solution)/shard_map/jit(cholesky)/cholesky | solution.py:172
  272.7 9.8 %custom-call.87 = f32[1,128,128]{1,2,0:T(8,128)S(1)} custom-call(f32[1,128,128]{2,1,0:T(8,128)S(1)} %get-tuple-element.67), custom_call_target="InvertDiagBlocksLowerTriangular" | custom-call | tf_op jit(solution)/shard_map/jit(cholesky)/cholesky | solution.py:172
  285.8 11.7 %cholesky.502 = f32[128,128]{1,0:T(8,128)S(1)} custom-call(f32[128,128]{1,0:T(8,128)S(1)} %cholesky.631), custom_call_target="Cholesky" | custom-call | tf_op jit(solution)/shard_map/jit(cholesky)/cholesky | solution.py:172
  298.8 9.8 %custom-call.88 = f32[1,128,128]{1,2,0:T(8,128)S(1)} custom-call(f32[1,128,128]{2,1,0:T(8,128)S(1)} %get-tuple-element.64), custom_call_target="InvertDiagBlocksLowerTriangular" | custom-call | tf_op jit(solution)/shard_map/jit(cholesky)/cholesky | solution.py:172
  312.1 11.9 %cholesky.521 = f32[128,128]{1,0:T(8,128)S(1)} custom-call(f32[128,128]{1,0:T(8,128)S(1)} %cholesky.636), custom_call_target="Cholesky" | custom-call | tf_op jit(solution)/shard_map/jit(cholesky)/cholesky | solution.py:172
  325.3 9.8 %custom-call.89 = f32[1,128,128]{1,2,0:T(8,128)S(1)} custom-call(f32[1,128,128]{2,1,0:T(8,128)S(1)} %get-tuple-element.61), custom_call_target="InvertDiagBlocksLowerTriangular" | custom-call | tf_op jit(solution)/shard_map/jit(cholesky)/cholesky | solution.py:172
  338.5 11.7 %cholesky.540 = f32[128,128]{1,0:T(8,128)S(1)} custom-call(f32[128,128]{1,0:T(8,128)S(1)} %cholesky.641), custom_call_target="Cholesky" | custom-call | tf_op jit(solution)/shard_map/jit(cholesky)/cholesky | solution.py:172
  351.5 10.2 %custom-call.90 = f32[1,128,128]{1,2,0:T(8,128)S(1)} custom-call(f32[1,128,128]{2,1,0:T(8,128)S(1)} %get-tuple-element.58), custom_call_target="InvertDiagBlocksLowerTriangular" | custom-call | tf_op jit(solution)/shard_map/jit(cholesky)/cholesky | solution.py:172
  365.0 11.7 %cholesky.560 = f32[128,128]{1,0:T(8,128)S(1)} custom-call(f32[128,128]{1,0:T(8,128)S(1)} %cholesky.646), custom_call_target="Cholesky" | custom-call | tf_op jit(solution)/shard_map/jit(cholesky)/cholesky | solution.py:172
  378.1 9.8 %custom-call.91 = f32[1,128,128]{1,2,0:T(8,128)S(1)} custom-call(f32[1,128,128]{2,1,0:T(8,128)S(1)} %get-tuple-element.55), custom_call_target="InvertDiagBlocksLowerTriangular" | custom-call | tf_op jit(solution)/shard_map/jit(cholesky)/cholesky | solution.py:172
  390.9 11.9 %cholesky.580 = f32[128,128]{1,0:T(8,128)S(1)} custom-call(f32[128,128]{1,0:T(8,128)S(1)} %cholesky.651), custom_call_target="Cholesky" | custom-call | tf_op jit(solution)/shard_map/jit(cholesky)/cholesky | solution.py:172
  404.0 9.8 %custom-call.92 = f32[1,128,128]{1,2,0:T(8,128)S(1)} custom-call(f32[1,128,128]{2,1,0:T(8,128)S(1)} %get-tuple-element.52), custom_call_target="InvertDiagBlocksLowerTriangular" | custom-call | tf_op jit(solution)/shard_map/jit(cholesky)/cholesky | solution.py:172
  416.5 11.7 %cholesky.598 = f32[128,128]{1,0:T(8,128)S(1)} custom-call(f32[128,128]{1,0:T(8,128)S(1)} %convolution_subtract_fusion.21), custom_call_target="Cholesky" | custom-call | tf_op jit(solution)/shard_map/jit(cholesky)/cholesky | solution.py:172
  439.9 28.2 %while.1 = (s32[]{:T(128)}, f32[1024,1024]{1,0:T(8,128)}, s32[8,2]{0,1:T(2,128)S(1)}, f32[8,128,128]{2,1,0:T(8,128)}, s32[]{:T(128)}) while((s32[]{:T(128)}, f32[1024,1024]{1,0:T(8,128)}, s32[8,2]{0,1:T(2,128)S(1)}, f32[8,128,128]{2,1,0:T(8,128)}, s32[]{:T(128)}) %tuple.84), condition=%wide.while_cond, body=%wide.while_body.sunk | while | flops 2 | bytes 132705 | solution.py:20
  468.1 79.6 %custom-call.93 = f32[8,128,128]{1,2,0:T(8,128)S(1)} custom-call(f32[8,128,128]{2,1,0:T(8,128)} %get-tuple-element.13), custom_call_target="InvertDiagBlocksLowerTriangular" | custom-call | tf_op jit(solution)/shard_map/jit(_solve_triangular)/triangular_solve | solution.py:20
  574.2 11.7 %custom-call.94 = f32[2,64,64]{2,1,0:T(8,128)S(1)} custom-call(f32[2,64,64]{2,1,0:T(8,128)S(1)} %fusion.264), custom_call_target="Cholesky" | custom-call | tf_op jit(solution)/shard_map/vmap(jit(cholesky))/cholesky | solution.py:60
  586.2 10.2 %custom-call.95 = f32[2,1,64,64]{2,3,1,0:T(8,128)S(1)} custom-call(f32[2,1,64,64]{3,2,1,0:T(8,128)S(1)} %select_bitcast_fusion), custom_call_target="InvertDiagBlocksLowerTriangular" | custom-call | tf_op jit(solution)/shard_map/vmap(jit(_solve_triangular))/triangular_solve | solution.py:61
  629.5 20.2 %fusion.23 = f32[3,64,1024]{2,1,0:T(8,128)S(1)} fusion(f32[3,1024,1024]{2,0,1:T(4,128)S(1)} %slice.592, f32[1024,64]{0,1:T(8,128)S(1)} %constant_dynamic-update-slice_fusion.36), kind=kOutput, calls=%fused_computation.33 | convolution fusion | flops 2415919104 | bytes 13631488 | tf_op jit(solution)/shard_map/aj,tij->tai/dot_general | solution.py:183
  (326 shorter events, 254.2 us)
Async XLA Ops:
  6.5 56.1 %all-gather.4.cloned.1.call-start = ((), (), s32[]{:S(2)}) async-start(), calls=%async_computation | async-start | bytes 2162688 | tf_op jit(solution)/shard_map/all_gather | solution.py:178
  8.0 114.1 %all-gather.6.cloned.1.call-start = ((), (), s32[]{:S(2)}) async-start(), calls=%async_computation.1 | async-start | bytes 4718592 | tf_op jit(solution)/shard_map/all_gather | solution.py:174
  10.0 195.1 %all-gather.8.cloned.1.call-start = ((), (), s32[]{:S(2)}) async-start(), calls=%async_computation.2 | async-start | bytes 17301504 | tf_op jit(solution)/shard_map/all_gather | solution.py:170
  20.2 5.9 copy-start.1
  66.9 504.7 %copy-start.15 = (f32[2,64,64]{2,1,0:T(8,128)}, f32[2,64,64]{2,1,0:T(8,128)S(1)}, u32[]{:S(2)}) copy-start(f32[2,64,64]{2,1,0:T(8,128)S(1)} %fusion.38) | copy-start | bytes 98308
  563.2 10.9 %copy-start.27 = (pred[64,64]{1,0:T(8,128)(4,1)S(1)}, pred[64,64]{1,0:T(8,128)(4,1)}, u32[]{:S(2)}) copy-start(pred[64,64]{1,0:T(8,128)(4,1)} %get-tuple-element.120) | copy-start | bytes 12292
  564.5 21.6 %copy-start.25 = (pred[64,64]{1,0:T(8,128)(4,1)S(1)}, pred[64,64]{1,0:T(8,128)(4,1)}, u32[]{:S(2)}) copy-start(pred[64,64]{1,0:T(8,128)(4,1)} %iota_compare_fusion.5) | copy-start | bytes 12292
  571.8 14.3 %copy-start.18 = (f32[2,64,64]{2,1,0:T(8,128)}, f32[2,64,64]{2,1,0:T(8,128)S(1)}, u32[]{:S(2)}) copy-start(f32[2,64,64]{2,1,0:T(8,128)S(1)} %fusion.331) | copy-start | bytes 98308
  585.9 23.7 %copy-start.20 = (f32[2,64,64]{2,1,0:T(8,128)}, f32[2,64,64]{2,1,0:T(8,128)S(1)}, u32[]{:S(2)}) copy-start(f32[2,64,64]{2,1,0:T(8,128)S(1)} %custom-call.94) | copy-start | bytes 98308
  596.4 11.8 %copy-start = (f32[1024,1024]{1,0:T(8,128)S(1)}, f32[1024,1024]{1,0:T(8,128)}, u32[]{:S(2)}) copy-start(f32[1024,1024]{1,0:T(8,128)} %get-tuple-element.169) | copy-start | bytes 12582916
  629.4 20.2 %copy-start.24 = (f32[2,64,64]{2,1,0:T(8,128)S(1)}, f32[2,64,64]{2,1,0:T(8,128)}, u32[]{:S(2)}) copy-start(f32[2,64,64]{2,1,0:T(8,128)} %fusion.54) | copy-start | bytes 98308
  629.4 21.8 %copy-start.23 = (f32[2,64,64]{2,1,0:T(8,128)S(1)}, f32[2,64,64]{2,1,0:T(8,128)}, u32[]{:S(2)}) copy-start(f32[2,64,64]{2,1,0:T(8,128)} %fusion.53) | copy-start | bytes 98308
  629.4 24.6 %copy-start.22 = (f32[2,64,64]{2,1,0:T(8,128)S(1)}, f32[2,64,64]{2,1,0:T(8,128)}, u32[]{:S(2)}) copy-start(f32[2,64,64]{2,1,0:T(8,128)} %fusion.52) | copy-start | bytes 98308
  649.6 6.5 copy-start.16
  651.2 8.1 %copy-start.11 = (f32[2,3,64,1024]{3,2,0,1:T(8,128)S(1)}, f32[2,3,64,1024]{3,2,0,1:T(8,128)}, u32[]{:S(2)}) copy-start(f32[2,3,64,1024]{3,2,0,1:T(8,128)} %get-tuple-element.28) | copy-start | bytes 4718596
  651.2 8.1 %copy-start.19 = (f32[2,64,64]{2,1,0:T(8,128)S(1)}, f32[2,64,64]{2,1,0:T(8,128)}, u32[]{:S(2)}) copy-start(f32[2,64,64]{2,1,0:T(8,128)} %copy-done.18) | copy-start | bytes 98308
  656.7 7.0 copy-start.7
  656.7 7.0 copy-start.9
  656.7 7.0 copy-start.14
  667.1 11.2 %copy-start.21 = (f32[2,64,64]{2,1,0:T(8,128)S(1)}, f32[2,64,64]{2,1,0:T(8,128)}, u32[]{:S(2)}) copy-start(f32[2,64,64]{2,1,0:T(8,128)} %copy-done.20) | copy-start | bytes 98308
  667.1 11.2 %copy-start.26 = (pred[64,64]{1,0:T(8,128)(4,1)S(1)}, pred[64,64]{1,0:T(8,128)(4,1)}, u32[]{:S(2)}) copy-start(pred[64,64]{1,0:T(8,128)(4,1)} %iota_compare_fusion.5) | copy-start | bytes 12292
  706.6 6.1 copy-start.10
  712.6 5.3 copy-start.8
  714.8 7.6 %copy-start.6 = (f32[2,3,64,1024]{3,2,0,1:T(8,128)S(1)}, f32[2,3,64,1024]{3,2,0,1:T(8,128)}, u32[]{:S(2)}) copy-start(f32[2,3,64,1024]{3,2,0,1:T(8,128)} %get-tuple-element.24) | copy-start | bytes 4718596
  (7 other events, 20.8 us)
Sparse Core Ops, SparseCore 0:
  9.9 52.7 all-gather.3
  64.4 57.7 all-gather.5
  124.7 80.3 all-gather.7
where the time goes:
time: 744 us; the launch traced here: 734 us
  other arithmetic  299 us (40%)
  waiting for transfers between devices  163 us (22%)
  matrix products  152 us (20%)
  local copies, waits for them, and re-layouts  98.7 us (13%)
  between operations  20.8 us (3%)
    another operation x30, other arithmetic, on_device(): lower_factor = jnp.linalg.cholesky(primal)  172 us
    another operation x3, other arithmetic, inverse_apply(): jax.scipy.linalg.solve_triangular(lower_factor, half_solved, lower=True,...  84.5 us
    all_gather x1, waiting for transfers between devices, on_device(): gathered = lax.all_gather(diag, 'row', axis=1, tiled=True)  74.5 us
    dot_general x48, matrix products, highest_accuracy(): jnp.dot(left, right, precision=HIGHEST_PRECISION, preferred_element_type=...  69.4 us
    all_gather x1, waiting for transfers between devices, on_device(): lax.all_gather(panel_rows, 'col', axis=3, tiled=True)  54 us
    all_gather x1, waiting for transfers between devices, on_device(): lax.all_gather(panel_cols, 'row', axis=2, tiled=True)  34 us
    another operation x24, local copies, waits for them, and re-layouts  28.2 us
    another operation x14, matrix products, on_device(): lower_factor = jnp.linalg.cholesky(primal)  22.9 us
  transfers between devices with their start and end apart: 3, of which 3 were waited for; matrix products, arithmetic and copies ran while one was open for 4% of the time, Pallas kernels for 0%

commit v1 on v0

--- a/solution.py
+++ b/solution.py
@@ -171,7 +171,9 @@
     primal = gathered[0]
     lower_factor = jnp.linalg.cholesky(primal)
     rows_kept = (
-        lax.all_gather(panel_rows, "col", axis=3, tiled=True)
+        jnp.concatenate(
+            lax.all_to_all(jnp.stack([panel_rows] * lax.axis_size("col")), "col", 0, 0), axis=3
+        )
         * rank_mask(panel_rank, rank_count)[:, None, :, None]
     )
     cols_kept = (

time: 744 us -> 682 us (0.917)
  waiting for transfers between devices: 163 us -> 90.9 us
  starting transfers between devices: 0.09 us -> 9.18 us
    all_gather x1, waiting for transfers between devices: 74.5 us -> 13.3 us  [on_device(): gathered = lax.all_gather(diag, 'row', axis=1, tiled=True)]
    all_gather x1 -> x0, waiting for transfers between devices: 54 us -> none  [on_device(): lax.all_gather(panel_rows, 'col', axis=3, tiled=True)]
    all_to_all x0 -> x1, waiting for transfers between devices: none -> 51.9 us  [on_device(): lax.all_to_all(jnp.stack([panel_rows] * lax.axis_size('col')), 'col', 0, 0)]
    all_to_all x0 -> x1, starting transfers between devices: none -> 9.13 us  [on_device(): lax.all_to_all(jnp.stack([panel_rows] * lax.axis_size('col')), 'col', 0, 0)]
    all_gather x1, waiting for transfers between devices: 34 us -> 25.7 us  [on_device(): lax.all_gather(panel_cols, 'row', axis=2, tiled=True)]
    another operation x24 -> x25, local copies, waits for them, and re-layouts: 28.2 us -> 30.7 us
    unnamed x96 -> x102, local copies, waits for them, and re-layouts: 21.9 us -> 21.1 us
  transfers between devices with their start and end apart: 3 -> 3, of which waited for: 3 -> 3; matrix products, arithmetic and copies ran while one was open for 4% -> 5% of each run, Pallas kernels for 0% -> 0%
where the time goes in v1:
time: 682 us; the launch traced here: 671 us
  other arithmetic  297 us (44%)
  matrix products  152 us (22%)
  local copies, waits for them, and re-layouts  100 us (15%)
  waiting for transfers between devices  90.9 us (13%)
  between operations  21.3 us (3%)
  starting transfers between devices  9.18 us (1%)
    another operation x30, other arithmetic, on_device(): lower_factor = jnp.linalg.cholesky(primal)  172 us
    another operation x3, other arithmetic, inverse_apply(): jax.scipy.linalg.solve_triangular(lower_factor, half_solved, lower=True,...  84.5 us
    dot_general x48, matrix products, highest_accuracy(): jnp.dot(left, right, precision=HIGHEST_PRECISION, preferred_element_type=...  69.4 us
    all_to_all x1, waiting for transfers between devices, on_device(): lax.all_to_all(jnp.stack([panel_rows] * lax.axis_size('col')), 'col', 0, 0)  51.9 us
    another operation x24, local copies, waits for them, and re-layouts  28.1 us
    all_gather x1, waiting for transfers between devices, on_device(): lax.all_gather(panel_cols, 'row', axis=2, tiled=True)  25.7 us
    another operation x14, matrix products, on_device(): lower_factor = jnp.linalg.cholesky(primal)  22.9 us
    unnamed x102, local copies, waits for them, and re-layouts  21.1 us
  transfers between devices with their start and end apart: 3, of which 3 were waited for; matrix products, arithmetic and copies ran while one was open for 5% of the time, Pallas kernels for 0%

profile of v1, /device:TPU:1, one launch (start us, length us, event | category | flops | bytes accessed | tf_op | source)
XLA Modules:
  0.0 671.5 jit_solution(11076455038036036455)
XLA Ops:
  36.9 25.7 %all-gather.3.cloned.1.call-done = f32[1,8,64,1024]{3,1,0,2:T(8,128)} async-done(((f32[1,8,2,1024]{3,1,0,2:T(8,128)}), f32[1,8,64,1024]{3,1,0,2:T(8,128)}) %all-gather.3.cloned.1.call-update) | async-done | bytes 2097168 | tf_op jit(solution)/shard_map/all_gather | solution.py:180
  68.1 51.9 %all-to-all-done = f32[8,2,8,64,128]{4,3,1,2,0:T(8,128)} async-done(((f32[8,2,8,64,128]{4,3,1,2,0:T(8,128)}), f32[8,2,8,64,128]{4,3,1,2,0:T(8,128)}, u32[]{:S(2)}, u32[]{:S(2)}) %all-to-all-start) | async-done | bytes 4194336 | tf_op jit(solution)/shard_map/all_to_all | solution.py:175
  128.9 13.3 %all-gather.5.cloned.1.call-done = f32[4,1024,1024]{2,0,1:T(4,128)} async-done(((f32[4,32,1024]{2,0,1:T(4,128)}), f32[4,1024,1024]{2,0,1:T(4,128)}) %all-gather.5.cloned.1.call-update) | async-done | bytes 16777232 | tf_op jit(solution)/shard_map/all_gather | solution.py:170
  150.9 11.4 %copy.217 = f32[1,1024,1024]{1,2,0:T(8,128)} copy(f32[1,1024,1024]{2,0,1:T(1,128)} %slice.584) | data formatting | bytes 8388608
  169.3 11.7 %cholesky.241 = f32[128,128]{1,0:T(8,128)S(1)} custom-call(f32[128,128]{1,0:T(8,128)S(1)} %cholesky.622), custom_call_target="Cholesky" | custom-call | tf_op jit(solution)/shard_map/jit(cholesky)/cholesky | solution.py:172
  181.0 9.8 %custom-call.86 = f32[1,128,128]{1,2,0:T(8,128)S(1)} custom-call(f32[1,128,128]{2,1,0:T(8,128)S(1)} %get-tuple-element.70), custom_call_target="InvertDiagBlocksLowerTriangular" | custom-call | tf_op jit(solution)/shard_map/jit(cholesky)/cholesky | solution.py:172
  197.2 11.8 %cholesky.264 = f32[128,128]{1,0:T(8,128)S(1)} custom-call(f32[128,128]{1,0:T(8,128)S(1)} %cholesky.626), custom_call_target="Cholesky" | custom-call | tf_op jit(solution)/shard_map/jit(cholesky)/cholesky | solution.py:172
  209.7 9.8 %custom-call.87 = f32[1,128,128]{1,2,0:T(8,128)S(1)} custom-call(f32[1,128,128]{2,1,0:T(8,128)S(1)} %get-tuple-element.67), custom_call_target="InvertDiagBlocksLowerTriangular" | custom-call | tf_op jit(solution)/shard_map/jit(cholesky)/cholesky | solution.py:172
  222.9 11.7 %cholesky.502 = f32[128,128]{1,0:T(8,128)S(1)} custom-call(f32[128,128]{1,0:T(8,128)S(1)} %cholesky.631), custom_call_target="Cholesky" | custom-call | tf_op jit(solution)/shard_map/jit(cholesky)/cholesky | solution.py:172
  235.9 9.8 %custom-call.88 = f32[1,128,128]{1,2,0:T(8,128)S(1)} custom-call(f32[1,128,128]{2,1,0:T(8,128)S(1)} %get-tuple-element.64), custom_call_target="InvertDiagBlocksLowerTriangular" | custom-call | tf_op jit(solution)/shard_map/jit(cholesky)/cholesky | solution.py:172
  249.2 11.9 %cholesky.521 = f32[128,128]{1,0:T(8,128)S(1)} custom-call(f32[128,128]{1,0:T(8,128)S(1)} %cholesky.636), custom_call_target="Cholesky" | custom-call | tf_op jit(solution)/shard_map/jit(cholesky)/cholesky | solution.py:172
  262.5 9.8 %custom-call.89 = f32[1,128,128]{1,2,0:T(8,128)S(1)} custom-call(f32[1,128,128]{2,1,0:T(8,128)S(1)} %get-tuple-element.61), custom_call_target="InvertDiagBlocksLowerTriangular" | custom-call | tf_op jit(solution)/shard_map/jit(cholesky)/cholesky | solution.py:172
  275.7 11.7 %cholesky.540 = f32[128,128]{1,0:T(8,128)S(1)} custom-call(f32[128,128]{1,0:T(8,128)S(1)} %cholesky.641), custom_call_target="Cholesky" | custom-call | tf_op jit(solution)/shard_map/jit(cholesky)/cholesky | solution.py:172
  288.7 10.2 %custom-call.90 = f32[1,128,128]{1,2,0:T(8,128)S(1)} custom-call(f32[1,128,128]{2,1,0:T(8,128)S(1)} %get-tuple-element.58), custom_call_target="InvertDiagBlocksLowerTriangular" | custom-call | tf_op jit(solution)/shard_map/jit(cholesky)/cholesky | solution.py:172
  302.2 11.7 %cholesky.560 = f32[128,128]{1,0:T(8,128)S(1)} custom-call(f32[128,128]{1,0:T(8,128)S(1)} %cholesky.646), custom_call_target="Cholesky" | custom-call | tf_op jit(solution)/shard_map/jit(cholesky)/cholesky | solution.py:172
  315.3 9.8 %custom-call.91 = f32[1,128,128]{1,2,0:T(8,128)S(1)} custom-call(f32[1,128,128]{2,1,0:T(8,128)S(1)} %get-tuple-element.55), custom_call_target="InvertDiagBlocksLowerTriangular" | custom-call | tf_op jit(solution)/shard_map/jit(cholesky)/cholesky | solution.py:172
  328.1 11.9 %cholesky.580 = f32[128,128]{1,0:T(8,128)S(1)} custom-call(f32[128,128]{1,0:T(8,128)S(1)} %cholesky.651), custom_call_target="Cholesky" | custom-call | tf_op jit(solution)/shard_map/jit(cholesky)/cholesky | solution.py:172
  341.3 9.8 %custom-call.92 = f32[1,128,128]{1,2,0:T(8,128)S(1)} custom-call(f32[1,128,128]{2,1,0:T(8,128)S(1)} %get-tuple-element.52), custom_call_target="InvertDiagBlocksLowerTriangular" | custom-call | tf_op jit(solution)/shard_map/jit(cholesky)/cholesky | solution.py:172
  353.7 11.7 %cholesky.598 = f32[128,128]{1,0:T(8,128)S(1)} custom-call(f32[128,128]{1,0:T(8,128)S(1)} %convolution_subtract_fusion.21), custom_call_target="Cholesky" | custom-call | tf_op jit(solution)/shard_map/jit(cholesky)/cholesky | solution.py:172
  377.3 28.1 %while.1 = (s32[]{:T(128)}, f32[1024,1024]{1,0:T(8,128)}, s32[8,2]{0,1:T(2,128)S(1)}, f32[8,128,128]{2,1,0:T(8,128)}, s32[]{:T(128)}) while((s32[]{:T(128)}, f32[1024,1024]{1,0:T(8,128)}, s32[8,2]{0,1:T(2,128)S(1)}, f32[8,128,128]{2,1,0:T(8,128)}, s32[]{:T(128)}) %tuple.84), condition=%wide.while_cond, body=%wide.while_body.sunk | while | flops 2 | bytes 132705 | solution.py:20
  405.4 79.6 %custom-call.93 = f32[8,128,128]{1,2,0:T(8,128)S(1)} custom-call(f32[8,128,128]{2,1,0:T(8,128)} %get-tuple-element.13), custom_call_target="InvertDiagBlocksLowerTriangular" | custom-call | tf_op jit(solution)/shard_map/jit(_solve_triangular)/triangular_solve | solution.py:20
  511.5 11.7 %custom-call.94 = f32[2,64,64]{2,1,0:T(8,128)S(1)} custom-call(f32[2,64,64]{2,1,0:T(8,128)S(1)} %fusion.264), custom_call_target="Cholesky" | custom-call | tf_op jit(solution)/shard_map/vmap(jit(cholesky))/cholesky | solution.py:60
  523.5 10.2 %custom-call.95 = f32[2,1,64,64]{2,3,1,0:T(8,128)S(1)} custom-call(f32[2,1,64,64]{3,2,1,0:T(8,128)S(1)} %select_bitcast_fusion), custom_call_target="InvertDiagBlocksLowerTriangular" | custom-call | tf_op jit(solution)/shard_map/vmap(jit(_solve_triangular))/triangular_solve | solution.py:61
  566.8 20.2 %fusion.23 = f32[3,64,1024]{2,1,0:T(8,128)S(1)} fusion(f32[3,1024,1024]{2,0,1:T(4,128)S(1)} %slice.592, f32[1024,64]{0,1:T(8,128)S(1)} %constant_dynamic-update-slice_fusion.36), kind=kOutput, calls=%fused_computation.33 | convolution fusion | flops 2415919104 | bytes 13631488 | tf_op jit(solution)/shard_map/aj,tij->tai/dot_general | solution.py:185
  (332 shorter events, 263.0 us)
Async XLA Ops:
  6.5 56.1 %all-gather.3.cloned.1.call-start = ((), (), s32[]{:S(2)}) async-start(), calls=%async_computation.1 | async-start | bytes 2162688 | tf_op jit(solution)/shard_map/all_gather | solution.py:180
  8.0 134.1 %all-gather.5.cloned.1.call-start = ((), (), s32[]{:S(2)}) async-start(), calls=%async_computation.2 | async-start | bytes 17301504 | tf_op jit(solution)/shard_map/all_gather | solution.py:170
  13.9 11.1 %copy-start.28 = (s32[2,1]{0,1:T(1,128)S(1)}, s32[2,1]{0,1:T(1,128)}, u32[]{:S(2)}) copy-start(s32[2,1]{0,1:T(1,128)} %param.19) | copy-start | bytes 28
  13.9 11.2 %copy-start.29 = (s32[2]{0:T(128)S(1)}, s32[2]{0:T(128)}, u32[]{:S(2)}) copy-start(s32[2]{0:T(128)} %param.16) | copy-start | bytes 28
  13.9 11.3 %copy-start.30 = (s32[2,1]{0,1:T(1,128)S(1)}, s32[2,1]{0,1:T(1,128)}, u32[]{:S(2)}) copy-start(s32[2,1]{0,1:T(1,128)} %param.18) | copy-start | bytes 28
  13.9 106.0 %all-to-all-start = ((f32[8,2,8,64,128]{4,3,1,2,0:T(8,128)}), f32[8,2,8,64,128]{4,3,1,2,0:T(8,128)}, u32[]{:S(2)}, u32[]{:S(2)}) async-start(f32[8,2,8,64,128]{4,3,1,2,0:T(8,128)} %stack.10), calls=%async_computation | async-start | bytes 8388608 | tf_op jit(solution)/shard_map/all_to_all | solution.py:175
  66.8 442.1 %copy-start.15 = (f32[2,64,64]{2,1,0:T(8,128)}, f32[2,64,64]{2,1,0:T(8,128)S(1)}, u32[]{:S(2)}) copy-start(f32[2,64,64]{2,1,0:T(8,128)S(1)} %fusion.38) | copy-start | bytes 98308
  500.6 10.9 %copy-start.27 = (pred[64,64]{1,0:T(8,128)(4,1)S(1)}, pred[64,64]{1,0:T(8,128)(4,1)}, u32[]{:S(2)}) copy-start(pred[64,64]{1,0:T(8,128)(4,1)} %get-tuple-element.120) | copy-start | bytes 12292
  501.9 21.6 %copy-start.25 = (pred[64,64]{1,0:T(8,128)(4,1)S(1)}, pred[64,64]{1,0:T(8,128)(4,1)}, u32[]{:S(2)}) copy-start(pred[64,64]{1,0:T(8,128)(4,1)} %iota_compare_fusion.5) | copy-start | bytes 12292
  509.1 14.3 %copy-start.18 = (f32[2,64,64]{2,1,0:T(8,128)}, f32[2,64,64]{2,1,0:T(8,128)S(1)}, u32[]{:S(2)}) copy-start(f32[2,64,64]{2,1,0:T(8,128)S(1)} %fusion.331) | copy-start | bytes 98308
  523.3 23.7 %copy-start.20 = (f32[2,64,64]{2,1,0:T(8,128)}, f32[2,64,64]{2,1,0:T(8,128)S(1)}, u32[]{:S(2)}) copy-start(f32[2,64,64]{2,1,0:T(8,128)S(1)} %custom-call.94) | copy-start | bytes 98308
  533.8 11.8 %copy-start = (f32[1024,1024]{1,0:T(8,128)S(1)}, f32[1024,1024]{1,0:T(8,128)}, u32[]{:S(2)}) copy-start(f32[1024,1024]{1,0:T(8,128)} %get-tuple-element.168) | copy-start | bytes 12582916
  566.8 20.2 %copy-start.24 = (f32[2,64,64]{2,1,0:T(8,128)S(1)}, f32[2,64,64]{2,1,0:T(8,128)}, u32[]{:S(2)}) copy-start(f32[2,64,64]{2,1,0:T(8,128)} %fusion.54) | copy-start | bytes 98308
  566.8 21.8 %copy-start.23 = (f32[2,64,64]{2,1,0:T(8,128)S(1)}, f32[2,64,64]{2,1,0:T(8,128)}, u32[]{:S(2)}) copy-start(f32[2,64,64]{2,1,0:T(8,128)} %fusion.53) | copy-start | bytes 98308
  566.8 24.6 %copy-start.22 = (f32[2,64,64]{2,1,0:T(8,128)S(1)}, f32[2,64,64]{2,1,0:T(8,128)}, u32[]{:S(2)}) copy-start(f32[2,64,64]{2,1,0:T(8,128)} %fusion.52) | copy-start | bytes 98308
  587.0 6.5 copy-start.16
  588.5 8.1 %copy-start.11 = (f32[2,3,64,1024]{3,2,0,1:T(8,128)S(1)}, f32[2,3,64,1024]{3,2,0,1:T(8,128)}, u32[]{:S(2)}) copy-start(f32[2,3,64,1024]{3,2,0,1:T(8,128)} %get-tuple-element.28) | copy-start | bytes 4718596
  588.6 8.1 %copy-start.19 = (f32[2,64,64]{2,1,0:T(8,128)S(1)}, f32[2,64,64]{2,1,0:T(8,128)}, u32[]{:S(2)}) copy-start(f32[2,64,64]{2,1,0:T(8,128)} %copy-done.18) | copy-start | bytes 98308
  594.1 7.0 %copy-start.7 = (f32[2,3,64,1024]{3,2,0,1:T(8,128)S(1)}, f32[2,3,64,1024]{3,2,0,1:T(8,128)}, u32[]{:S(2)}) copy-start(f32[2,3,64,1024]{3,2,0,1:T(8,128)} %get-tuple-element.27) | copy-start | bytes 4718596
  594.1 7.0 %copy-start.9 = (f32[2,64,3,1024]{3,1,2,0:T(8,128)S(1)}, f32[2,64,3,1024]{3,1,2,0:T(8,128)}, u32[]{:S(2)}) copy-start(f32[2,64,3,1024]{3,1,2,0:T(8,128)} %fusion.64) | copy-start | bytes 4718596
  594.1 7.0 %copy-start.14 = (f32[2,64,64]{2,1,0:T(8,128)S(1)}, f32[2,64,64]{2,1,0:T(8,128)}, u32[]{:S(2)}) copy-start(f32[2,64,64]{2,1,0:T(8,128)} %copy-done.13) | copy-start | bytes 98308
  604.4 11.2 %copy-start.21 = (f32[2,64,64]{2,1,0:T(8,128)S(1)}, f32[2,64,64]{2,1,0:T(8,128)}, u32[]{:S(2)}) copy-start(f32[2,64,64]{2,1,0:T(8,128)} %copy-done.20) | copy-start | bytes 98308
  604.4 11.2 %copy-start.26 = (pred[64,64]{1,0:T(8,128)(4,1)S(1)}, pred[64,64]{1,0:T(8,128)(4,1)}, u32[]{:S(2)}) copy-start(pred[64,64]{1,0:T(8,128)(4,1)} %iota_compare_fusion.5) | copy-start | bytes 12292
  652.2 7.6 %copy-start.6 = (f32[2,3,64,1024]{3,2,0,1:T(8,128)S(1)}, f32[2,3,64,1024]{3,2,0,1:T(8,128)}, u32[]{:S(2)}) copy-start(f32[2,3,64,1024]{3,2,0,1:T(8,128)} %get-tuple-element.24) | copy-start | bytes 4718596
  (10 other events, 38.1 us)
Sparse Core Ops, SparseCore 0:
  9.9 52.6 all-gather.2
  65.2 76.9 all-gather.4
